TPU v7x, 256 devices: a whole 4x4x8 slice. The times are simulated.
256 devices in a mesh: sec: 4 (over z_lo, core), lat: 16 (over x, y), col: 4 (over z_hi).
Axes of the slice: x: 4, y: 4, z: 8 (z_hi: 4, z_lo: 2; z = z_hi * 2 + z_lo), core: 2. Of those that a mesh axis runs over, the one named last changes fastest.
Arguments:
- state: float32 [1, 4, 28, 192, 384], P(None, 'sec', None, 'lat', 'col'), may hold values from -6 to 6
- forcing: float32 [1, 4, 28, 192, 384], P(None, 'sec', None, 'lat', 'col'), may hold values from -4 to 4
- crm_moisture: bfloat16 [1, 32, 28, 64, 4, 288], P(None, None, None, ('sec', 'lat'), 'col'), may hold values from -6 to 6
- cloud_order: int32 [4, 16, 1152], P('col', 'lat'), may hold values from 0 to 1151, each once within a row
- wave_table: int32 [128], replicated, may hold values from 0 to 127, each once
Outputs:
- state_out: float32 [1, 4, 28, 192, 384], P(None, 'sec', None, 'lat', 'col')
- spectral: float32 [4, 1, 28, 128, 2, 128], P('sec', None, 'col', 'lat')
Inputs may be any that keep to these rules, and one draw needn't show every extreme that they name: `cloud_order`: every row lists each of the 1152 columns of a band block once. `wave_table`: each wavenumber stands in exactly one slot.
All inputs are finite; a program needn't handle non-finite values.
Results may differ from a plain program's by a relative error of at most 0.0003.
Values sent between devices are 32-bit elements; how exact they have to be, the bound alone decides.
No kernel may reach another device: no remote copies, remote signals or barrier semaphores. Data moves between devices by JAX's collectives and lax.ppermute only.
A program may use at most 64 MiB of HBM per device.

v0:
```python
import math
import jax
import jax.numpy as jnp
from jax import lax
from jax.sharding import PartitionSpec as P

NLON = 384
NLAT = 192
MMAX = 128
NSUB = 4
COURANT_SCALE = 0.4
CONDENSE = 0.5


def transport(values, courant, mixing):
    forward = jnp.roll(values, -1, axis=0)
    behind = jnp.roll(values, 1, axis=0)
    return -0.5 * courant * (forward - behind) + mixing * (forward - 2.0 * values + behind)


def cloud_model(vertical_state_stack, forcing, vapour_mass_fraction):
    wind_u = vertical_state_stack[0]
    wind_v = vertical_state_stack[1]
    atmospheric_warmth = vertical_state_stack[2]
    humidity = vertical_state_stack[3]
    courant = COURANT_SCALE * jnp.tanh(wind_u)
    mixing = 0.2 + 0.5 * jnp.abs(courant)
    convective_warming_rate = jnp.broadcast_to(atmospheric_warmth, vapour_mass_fraction.shape)
    crm_water = humidity + vapour_mass_fraction
    start_water = crm_water
    ground_precipitation = jnp.zeros_like(atmospheric_warmth)
    for substep in range(NSUB):
        heat_move = transport(convective_warming_rate, courant, mixing)
        water_move = transport(crm_water, courant, mixing)
        condensed = CONDENSE * jnp.maximum(crm_water - convective_warming_rate, 0.0)
        convective_warming_rate = (
            convective_warming_rate + heat_move + condensed + forcing[2] / NSUB
        )
        crm_water = crm_water + water_move - condensed + forcing[3] / NSUB
        ground_precipitation = ground_precipitation + jnp.mean(condensed, axis=0)
    ground_precipitation = ground_precipitation / NSUB
    zonal_velocity_rate = -ground_precipitation * wind_u + forcing[0]
    meridional_velocity_rate = -ground_precipitation * wind_v + forcing[1]
    warming_rate_change = jnp.mean(convective_warming_rate, axis=0) - atmospheric_warmth
    vapour_rate_change = jnp.mean(crm_water - start_water, axis=0)
    return jnp.stack(
        (zonal_velocity_rate, meridional_velocity_rate, warming_rate_change, vapour_rate_change)
    )


def trig_table(longitudes, wave_numbers):
    phase = (longitudes[:, None] * wave_numbers[None, :] % NLON).astype(jnp.float32) * (
        2.0 * math.pi / NLON
    )
    return jnp.stack((jnp.cos(phase), jnp.sin(phase)), axis=1) / math.sqrt(NLON)


def legendre_table(orders):
    colatitude = (jnp.arange(NLAT, dtype=jnp.int32).astype(jnp.float32) + 0.5) * (math.pi / NLAT)
    cosine = jnp.cos(colatitude)[None, :]
    sine_lat = jnp.sin(colatitude)
    order_col = orders.astype(jnp.float32)[:, None]
    log_diag = 0.5 * (
        lax.lgamma(order_col + 1.5) - lax.lgamma(jnp.float32(1.5)) - lax.lgamma(order_col + 1.0)
    )
    log_diag = log_diag + order_col * jnp.log(sine_lat)[None, :] - 0.5 * math.log(2.0)
    diagonal = jnp.exp(log_diag)
    empty = jnp.zeros_like(diagonal)

    def march_forward(carried, degree):
        previous, current = carried
        deg_float = degree.astype(jnp.float32)
        active = deg_float > order_col
        numerator = jnp.where(active, 4.0 * deg_float * deg_float - 1.0, 1.0)
        bottom = jnp.where(active, deg_float * deg_float - order_col * order_col, 1.0)
        lower_deg = deg_float - 1.0
        retreat = jnp.sqrt(
            jnp.maximum(lower_deg * lower_deg - order_col * order_col, 0.0)
            / (4.0 * lower_deg * lower_deg - 1.0)
        )
        grown = jnp.sqrt(numerator / bottom) * (cosine * current - retreat * previous)
        fresh_row = jnp.where(active, grown, jnp.where(deg_float == order_col, diagonal, 0.0))
        return ((current, fresh_row), fresh_row)

    _, legendre_rows = lax.scan(
        march_forward, (empty, empty), jnp.arange(MMAX, dtype=jnp.int32), unroll=8
    )
    weights = sine_lat / math.sqrt(NLAT)
    return legendre_rows * weights[None, None, :]


def shards(state, forcing, crm_moisture, cloud_order, wave_table):
    members, _, levels, band_rows, lon_block = state.shape
    sections = lax.axis_size("sec")
    lat_bands = lax.axis_size("lat")
    block_cols = band_rows * lon_block
    targets = sections * lat_bands
    per_target = block_cols // targets
    run_cols = lat_bands * per_target
    slot_list = cloud_order[0, 0]
    flat_state = state[:, 0].reshape(members, levels, block_cols)
    flat_force = forcing[:, 0].reshape(members, levels, block_cols)
    stacked = jnp.stack((flat_state, flat_force))
    column_ids = jnp.arange(block_cols, dtype=jnp.int32)
    selector = (slot_list[:, None] == column_ids[None, :]).astype(jnp.float32)
    selector = selector.reshape(targets, per_target, block_cols)
    by_target = jnp.einsum("xelc,tpc->txelp", stacked, selector, precision=lax.Precision.HIGHEST)
    send_width = 2 * members * levels * per_target
    outgoing = by_target.reshape(targets, 1, send_width)
    arrived = lax.all_to_all(outgoing, ("sec", "lat"), split_axis=0, concat_axis=1, tiled=True)
    arrived = arrived.reshape(sections, lat_bands, 2, members, levels, per_target)
    arrived = arrived.transpose(2, 3, 0, 4, 1, 5).reshape(2, members, sections, levels, run_cols)
    vapour_mass_fraction = crm_moisture[:, :, :, 0, 0, :].astype(jnp.float32)
    tendency = jax.vmap(cloud_model)(arrived[0], arrived[1], vapour_mass_fraction)
    back_width = members * levels * per_target
    parted = tendency.reshape(members, sections, levels, lat_bands, per_target).transpose(
        1, 3, 0, 2, 4
    )
    homeward = parted.reshape(targets, 1, back_width)
    returned = lax.all_to_all(homeward, ("sec", "lat"), split_axis=0, concat_axis=1, tiled=True)
    returned = returned.reshape(targets, members, levels, per_target)
    column_tend = jnp.einsum("telp,tpc->elc", returned, selector, precision=lax.Precision.HIGHEST)
    new_state = state + column_tend.reshape(members, 1, levels, band_rows, lon_block)
    fields_now = new_state[:, 0]
    lon_start = lax.axis_index("col") * lon_block
    trig_rows = trig_table(lon_start + jnp.arange(lon_block, dtype=jnp.int32), wave_table)
    spectra = lax.psum_scatter(
        jnp.einsum("elay,ycs->leacs", fields_now, trig_rows, precision=lax.Precision.HIGHEST),
        "col",
        scatter_dimension=0,
        tiled=True,
    )
    owner_count = MMAX // lat_bands
    owned_waves = lax.dynamic_slice_in_dim(
        wave_table, lax.axis_index("lat") * owner_count, owner_count
    )
    weighted = legendre_table(owned_waves)
    coeffs = jnp.einsum(
        "leacs,nsa->lescn",
        lax.all_to_all(spectra, "lat", split_axis=4, concat_axis=2, tiled=True),
        weighted,
        precision=lax.Precision.HIGHEST,
    )
    return (new_state, coeffs.transpose(1, 0, 2, 3, 4)[None])


def solution(mesh):
    placed = (
        P(None, "sec", None, "lat", "col"),
        P(None, "sec", None, "lat", "col"),
        P(None, None, None, ("sec", "lat"), "col", None),
        P("col", "lat", None),
        P(),
    )
    return jax.shard_map(
        shards,
        mesh=mesh,
        in_specs=placed,
        out_specs=(P(None, "sec", None, "lat", "col"), P("sec", None, "col", "lat", None, None)),
        check_vma=False,
    )
```

profile of v0, /device:TPU:64, one launch (start us, length us, event | category | flops | bytes accessed | tf_op | source)
XLA Modules:
  0.0 213.8 jit_solution(3303707262347530788)
XLA Ops:
  7.2 0.7 reduce.6
  8.1 1.4 reduce.8
  9.6 1.4 reduce.7
  11.0 4.3 %fusion.56 = f32[64,2,1,28,18]{0,3,1,4,2:T(8,128)S(1)} fusion(s32[64,18]{0,1:T(8,128)S(1)} %copy.55, f32[1,1,28,1152]{3,2,0,1:T(8,128)S(1)} %stack_reshape_squeeze.9, f32[1,1,28,1152]{3,2,0,1:T(8,128)S(1)} %stack_reshape_squeeze.8), kind=kOutput, calls=%fused_computation.126 | convolution fusion | flops 893205504 | bytes 520704 | tf_op jit(solution)/shard_map/xelc,tpc->txelp/dot_general | solution.py:107
  15.9 1.3 copy.59
  17.3 9.5 %all-to-all-start = ((f32[64,1,1008]{2,1,0:T(1,128)}), f32[64,1,1008]{2,1,0:T(1,128)S(1)}, u32[]{:S(2)}, u32[]{:S(2)}) async-start(f32[64,1,1008]{2,1,0:T(1,128)} %copy.59), calls=%async_computation | async-start | bytes 524288 | tf_op jit(solution)/shard_map/all_to_all | solution.py:110
  27.0 9.4 %all-to-all-done = f32[64,1,1008]{2,1,0:T(1,128)S(1)} async-done(((f32[64,1,1008]{2,1,0:T(1,128)}), f32[64,1,1008]{2,1,0:T(1,128)S(1)}, u32[]{:S(2)}, u32[]{:S(2)}) %all-to-all-start) | async-done | bytes 258080 | tf_op jit(solution)/shard_map/all_to_all | solution.py:110
  36.4 0.6 reduce.9
  37.0 2.1 reshape.4329
  41.8 0.7 copy-done
  42.6 0.9 fusion.52
  43.8 2.9 %fusion.65 = (f32[28,288]{1,0:T(8,128)S(1)}, f32[28,288]{1,0:T(8,128)S(1)}, f32[1,32,28,288]{3,1,2,0:T(8,128)S(1)}) fusion(f32[28,288]{1,0:T(8,128)S(1)} %get-tuple-element.406, bf16[1,32,28,1,1,288]{5,1,4,3,2,0:T(8,128)(2,1)S(1)} %copy-done, f32[28,288]{1,0:T(8,128)S(1)} %get-tuple-element.411, f32[28,288]{1,0:T(8,128)S(1)} %broadcast_multiply_fusion.2, ...), kind=kLoop, calls=%fused_computation.133 | loop fusion | flops 8499456 | bytes 4935168 | tf_op jit(solution)/shard_map/vmap()/reduce_sum | solution.py:40
  47.3 3.4 %fusion.66 = (f32[28,288]{1,0:T(8,128)S(1)}, f32[1,32,28,288]{3,1,2,0:T(8,128)S(1)}, f32[1,32,28,288]{3,1,2,0:T(8,128)S(1)}) fusion(f32[28,288]{1,0:T(8,128)S(1)} %get-tuple-element.407, f32[1,32,28,288]{3,1,2,0:T(8,128)S(1)} %get-tuple-element.324, f32[28,288]{1,0:T(8,128)S(1)} %get-tuple-element.406, bf16[1,32,28,1,1,288]{5,1,4,3,2,0:T(8,128)(2,1)S(1)} %copy-done, ...), kind=kLoop, calls=%fused_computation.134 | loop fusion | flops 12120192 | bytes 9031680 | tf_op jit(solution)/shard_map/vmap()/reduce_sum | solution.py:40
  51.5 2.0 subtract_add_fusion
  54.1 3.1 %add_reduce_fusion = (f32[28,288]{1,0:T(8,128)S(1)}, f32[28,288]{1,0:T(8,128)S(1)}, f32[28,288]{1,0:T(8,128)S(1)}) fusion(f32[1,32,28,288]{3,1,2,0:T(8,128)S(1)} %get-tuple-element.365, f32[1,31,28,288]{3,1,2,0:T(8,128)S(1)} %get-tuple-element.377, f32[1,1,28,288]{3,1,2,0:T(1,128)S(1)} %get-tuple-element.379, f32[1,1,28,288]{3,1,2,0:T(1,128)S(1)} %get-tuple-element.378, ...), kind=kLoop, calls=%fused_computation.115 | loop fusion | flops 8491392 | bytes 6967296 | tf_op jit(solution)/shard_map/vmap()/reduce_sum | solution.py:44
  59.0 1.9 reshape.4347
  60.8 4.6 %all-to-all-start.1 = ((f32[64,1,504]{2,1,0:T(1,128)}), f32[64,1,504]{2,1,0:T(1,128)S(1)}, u32[]{:S(2)}, u32[]{:S(2)}) async-start(f32[64,1,504]{2,1,0:T(1,128)} %reshape.4347), calls=%async_computation.1 | async-start | bytes 262144 | tf_op jit(solution)/shard_map/all_to_all | solution.py:120
  65.9 8.1 %all-to-all-done.1 = f32[64,1,504]{2,1,0:T(1,128)S(1)} async-done(((f32[64,1,504]{2,1,0:T(1,128)}), f32[64,1,504]{2,1,0:T(1,128)S(1)}, u32[]{:S(2)}, u32[]{:S(2)}) %all-to-all-start.1) | async-done | bytes 129056 | tf_op jit(solution)/shard_map/all_to_all | solution.py:120
  74.2 2.5 %fusion.62 = f32[1,1,28,12,96]{4,2,3,1,0:T(8,128)S(1)} fusion(s32[12,96]{1,0:T(8,128)S(1)} %multiply_add_fusion.1, s32[18,64]{1,0:T(8,128)S(1)} %copy.67, f32[64,28,18]{0,2,1:T(8,128)S(1)} %reshape.4331, f32[1,1,28,12,96]{4,1,3,2,0:T(1,128)S(1)} %copy-done.1), kind=kOutput, calls=%fused_computation.129 | convolution fusion | flops 447266304 | bytes 396288 | tf_op jit(solution)/shard_map/telp,tpc->elc/dot_general | solution.py:122
  77.1 1.0 copy.70
  78.2 106.6 %while.19 = (s32[]{:T(128)}, f32[8,192]{1,0:T(8,128)S(1)}, f32[8,192]{1,0:T(8,128)S(1)}, f32[16,8,8,192]{3,2,1,0:T(8,128)S(1)}, s32[16,8]{0,1:T(8,128)S(1)}, /*i...) while((s32[]{:T(128)}, f32[8,192]{1,0:T(8,128)S(1)}, ...), condition=%wide.region_7.8_spmd.clone.clone, body=%wide.region_6.7_spmd.clone.clone.sunk | while | flops 228562 | bytes 435795 | solution.py:85
  98.2 0.6 fusion.125
  186.7 0.9 constant_dynamic-slice_fusion.1
  187.6 1.1 copy.71
  188.7 2.0 reshape.4361
  190.7 3.8 %all-to-all-start.2 = ((f32[16,1,1344]{2,1,0:T(1,128)}), f32[16,1,1344]{2,1,0:T(1,128)S(1)}, u32[]{:S(2)}, u32[]{:S(2)}) async-start(f32[16,1,1344]{2,1,0:T(1,128)} %reshape.4361), calls=%async_computation.2 | async-start | bytes 180224 | tf_op jit(solution)/shard_map/all_to_all | solution.py:140
  194.5 0.9 copy.75
  195.4 6.5 %all-to-all-done.2 = f32[16,1,1344]{2,1,0:T(1,128)S(1)} async-done(((f32[16,1,1344]{2,1,0:T(1,128)}), f32[16,1,1344]{2,1,0:T(1,128)S(1)}, u32[]{:S(2)}, u32[]{:S(2)}) %all-to-all-start.2) | async-done | bytes 86048 | tf_op jit(solution)/shard_map/all_to_all | solution.py:140
  202.4 0.9 reduce.16
  203.2 1.4 reshape.4362
  205.4 0.9 convolution_bitcast_fusion.1
  206.3 0.7 copy.76
  (326 shorter events, 35.4 us)
Async XLA Ops:
  15.4 11.4 %copy-start.2 = (s32[128]{0:T(128)S(1)}, s32[128]{0:T(128)}, u32[]{:S(2)}) copy-start(s32[128]{0:T(128)} %param.11) | copy-start | bytes 1540
  17.3 19.1 %all-to-all-start = ((f32[64,1,1008]{2,1,0:T(1,128)}), f32[64,1,1008]{2,1,0:T(1,128)S(1)}, u32[]{:S(2)}, u32[]{:S(2)}) async-start(f32[64,1,1008]{2,1,0:T(1,128)} %copy.59), calls=%async_computation | async-start | bytes 524288 | tf_op jit(solution)/shard_map/all_to_all | solution.py:110
  41.5 1.1 copy-start
  59.0 15.2 %copy-start.1 = (f32[1,1,28,12,96]{4,1,3,2,0:T(1,128)S(1)}, f32[1,1,28,12,96]{4,1,3,2,0:T(1,128)}, u32[]{:S(2)}) copy-start(f32[1,1,28,12,96]{4,1,3,2,0:T(1,128)} %param.7) | copy-start | bytes 387076
  60.8 13.2 %all-to-all-start.1 = ((f32[64,1,504]{2,1,0:T(1,128)}), f32[64,1,504]{2,1,0:T(1,128)S(1)}, u32[]{:S(2)}, u32[]{:S(2)}) async-start(f32[64,1,504]{2,1,0:T(1,128)} %reshape.4347), calls=%async_computation.1 | async-start | bytes 262144 | tf_op jit(solution)/shard_map/all_to_all | solution.py:120
  65.5 121.2 %all-reduce.3.cloned.1.call-start = ((), (), s32[]{:S(2)}) async-start(), calls=%async_computation.3 | async-start | bytes 688128
  184.7 0.7 copy-start.3
  190.7 11.2 %all-to-all-start.2 = ((f32[16,1,1344]{2,1,0:T(1,128)}), f32[16,1,1344]{2,1,0:T(1,128)S(1)}, u32[]{:S(2)}, u32[]{:S(2)}) async-start(f32[16,1,1344]{2,1,0:T(1,128)} %reshape.4361), calls=%async_computation.2 | async-start | bytes 180224 | tf_op jit(solution)/shard_map/all_to_all | solution.py:140
Sparse Core Ops, SparseCore 0:
  78.3 49.5 all-reduce.2
where the time goes:
time: 215 us; the launch traced here: 214 us
  loops' own time  82 us (38%)
  local copies, waits for them, and re-layouts  34.4 us (16%)
  other arithmetic  32.1 us (15%)
  waiting for transfers between devices  24 us (11%)
  starting transfers between devices  17.9 us (8%)
  between operations  15.2 us (7%)
  matrix products  8.2 us (4%)
    another operation x1, loops' own time, legendre_table(): lax.scan(march_forward, (empty, empty), jnp.arange(MMAX, dtype=jnp.int32)...  82 us
    while x112, other arithmetic  9.89 us
    slice x16, local copies, waits for them, and re-layouts, legendre_table(): lax.scan(march_forward, (empty, empty), jnp.arange(MMAX, dtype=jnp.int32)...  9.64 us
    all_to_all x1, starting transfers between devices, shards(): lax.all_to_all(outgoing, ('sec', 'lat'), split_axis=0, concat_axis=1, til...  9.47 us
    all_to_all x1, waiting for transfers between devices, shards(): lax.all_to_all(outgoing, ('sec', 'lat'), split_axis=0, concat_axis=1, til...  9.4 us
    all_to_all x1, waiting for transfers between devices, shards(): lax.all_to_all(homeward, ('sec', 'lat'), split_axis=0, concat_axis=1, til...  8.07 us
    unnamed x17, local copies, waits for them, and re-layouts  7.45 us
    all_to_all x1, waiting for transfers between devices, shards(): lax.all_to_all(spectra, 'lat', split_axis=4, concat_axis=2, tiled=True)  6.49 us
  transfers between devices with their start and end apart: 4, of which 3 were waited for; matrix products, arithmetic and copies ran while one was open for 13% of the time, Pallas kernels for 0%

commit v1 on v0

--- a/solution.py
+++ b/solution.py
@@ -137,7 +137,12 @@
     weighted = legendre_table(owned_waves)
     coeffs = jnp.einsum(
         "leacs,nsa->lescn",
-        lax.all_to_all(spectra, "lat", split_axis=4, concat_axis=2, tiled=True),
+        jnp.concatenate(
+            lax.all_to_all(
+                jnp.stack(jnp.split(spectra, lax.axis_size("lat"), axis=4)), "lat", 0, 0
+            ),
+            axis=2,
+        ),
         weighted,
         precision=lax.Precision.HIGHEST,
     )

time: 215 us -> 220 us (1.023)
  local copies, waits for them, and re-layouts: 34.4 us -> 39 us
    another operation x2 -> x5, local copies, waits for them, and re-layouts: 0.46 us -> 5.29 us  [the longest x2 4.54 us: shards(): jnp.stack(jnp.split(spectra, lax.axis_size('lat'), axis=4))]
    unnamed x17 -> x31, local copies, waits for them, and re-layouts: 7.45 us -> 7.55 us
  transfers between devices with their start and end apart: 4 -> 4, of which waited for: 3 -> 3; matrix products, arithmetic and copies ran while one was open for 13% -> 12% of each run, Pallas kernels for 0% -> 0%
where the time goes in v1:
time: 220 us; the launch traced here: 218 us
  loops' own time  82 us (37%)
  local copies, waits for them, and re-layouts  39 us (18%)
  other arithmetic  32.1 us (15%)
  waiting for transfers between devices  24 us (11%)
  starting transfers between devices  17.9 us (8%)
  between operations  15.3 us (7%)
  matrix products  8.16 us (4%)
    another operation x1, loops' own time, legendre_table(): lax.scan(march_forward, (empty, empty), jnp.arange(MMAX, dtype=jnp.int32)...  82 us
    while x112, other arithmetic  9.89 us
    slice x16, local copies, waits for them, and re-layouts, legendre_table(): lax.scan(march_forward, (empty, empty), jnp.arange(MMAX, dtype=jnp.int32)...  9.64 us
    all_to_all x1, starting transfers between devices, shards(): lax.all_to_all(outgoing, ('sec', 'lat'), split_axis=0, concat_axis=1, til...  9.47 us
    all_to_all x1, waiting for transfers between devices, shards(): lax.all_to_all(outgoing, ('sec', 'lat'), split_axis=0, concat_axis=1, til...  9.4 us
    all_to_all x1, waiting for transfers between devices, shards(): lax.all_to_all(homeward, ('sec', 'lat'), split_axis=0, concat_axis=1, til...  8.07 us
    unnamed x31, local copies, waits for them, and re-layouts  7.55 us
    all_to_all x1, waiting for transfers between devices, shards(): lax.all_to_all(jnp.stack(jnp.split(spectra, lax.axis_size('lat'), axis=4)...  6.49 us
  transfers between devices with their start and end apart: 4, of which 3 were waited for; matrix products, arithmetic and copies ran while one was open for 12% of the time, Pallas kernels for 0%

profile of v1, /device:TPU:64, one launch (start us, length us, event | category | flops | bytes accessed | tf_op | source)
XLA Modules:
  0.0 218.4 jit_solution(2704078839624187403)
XLA Ops:
  7.2 0.7 reduce.6
  8.1 1.4 reduce.8
  9.6 1.4 reduce.7
  11.0 4.3 %fusion.56 = f32[64,2,1,28,18]{0,3,1,4,2:T(8,128)S(1)} fusion(s32[64,18]{0,1:T(8,128)S(1)} %copy.68, f32[1,1,28,1152]{3,2,0,1:T(8,128)S(1)} %stack_reshape_squeeze.9, f32[1,1,28,1152]{3,2,0,1:T(8,128)S(1)} %stack_reshape_squeeze.8), kind=kOutput, calls=%fused_computation.126 | convolution fusion | flops 893205504 | bytes 520704 | tf_op jit(solution)/shard_map/xelc,tpc->txelp/dot_general | solution.py:107
  15.9 1.3 copy.72
  17.3 9.5 %all-to-all-start = ((f32[64,1,1008]{2,1,0:T(1,128)}), f32[64,1,1008]{2,1,0:T(1,128)S(1)}, u32[]{:S(2)}, u32[]{:S(2)}) async-start(f32[64,1,1008]{2,1,0:T(1,128)} %copy.72), calls=%async_computation | async-start | bytes 524288 | tf_op jit(solution)/shard_map/all_to_all | solution.py:110
  27.0 9.4 %all-to-all-done = f32[64,1,1008]{2,1,0:T(1,128)S(1)} async-done(((f32[64,1,1008]{2,1,0:T(1,128)}), f32[64,1,1008]{2,1,0:T(1,128)S(1)}, u32[]{:S(2)}, u32[]{:S(2)}) %all-to-all-start) | async-done | bytes 258080 | tf_op jit(solution)/shard_map/all_to_all | solution.py:110
  36.4 0.6 reduce.9
  37.0 2.1 reshape.4333
  41.8 0.7 copy-done
  42.6 0.9 fusion.52
  43.8 2.9 %fusion.65 = (f32[28,288]{1,0:T(8,128)S(1)}, f32[28,288]{1,0:T(8,128)S(1)}, f32[1,32,28,288]{3,1,2,0:T(8,128)S(1)}) fusion(f32[28,288]{1,0:T(8,128)S(1)} %get-tuple-element.406, bf16[1,32,28,1,1,288]{5,1,4,3,2,0:T(8,128)(2,1)S(1)} %copy-done, f32[28,288]{1,0:T(8,128)S(1)} %get-tuple-element.411, f32[28,288]{1,0:T(8,128)S(1)} %broadcast_multiply_fusion.2, ...), kind=kLoop, calls=%fused_computation.132 | loop fusion | flops 8499456 | bytes 4935168 | tf_op jit(solution)/shard_map/vmap()/reduce_sum | solution.py:40
  47.3 3.4 %fusion.66 = (f32[28,288]{1,0:T(8,128)S(1)}, f32[1,32,28,288]{3,1,2,0:T(8,128)S(1)}, f32[1,32,28,288]{3,1,2,0:T(8,128)S(1)}) fusion(f32[28,288]{1,0:T(8,128)S(1)} %get-tuple-element.407, f32[1,32,28,288]{3,1,2,0:T(8,128)S(1)} %get-tuple-element.324, f32[28,288]{1,0:T(8,128)S(1)} %get-tuple-element.406, bf16[1,32,28,1,1,288]{5,1,4,3,2,0:T(8,128)(2,1)S(1)} %copy-done, ...), kind=kLoop, calls=%fused_computation.133 | loop fusion | flops 12120192 | bytes 9031680 | tf_op jit(solution)/shard_map/vmap()/reduce_sum | solution.py:40
  51.5 2.0 subtract_add_fusion
  54.1 3.1 %add_reduce_fusion = (f32[28,288]{1,0:T(8,128)S(1)}, f32[28,288]{1,0:T(8,128)S(1)}, f32[28,288]{1,0:T(8,128)S(1)}) fusion(f32[1,32,28,288]{3,1,2,0:T(8,128)S(1)} %get-tuple-element.365, f32[1,31,28,288]{3,1,2,0:T(8,128)S(1)} %get-tuple-element.377, f32[1,1,28,288]{3,1,2,0:T(1,128)S(1)} %get-tuple-element.379, f32[1,1,28,288]{3,1,2,0:T(1,128)S(1)} %get-tuple-element.378, ...), kind=kLoop, calls=%fused_computation.115 | loop fusion | flops 8491392 | bytes 6967296 | tf_op jit(solution)/shard_map/vmap()/reduce_sum | solution.py:44
  59.0 1.9 reshape.4352
  60.8 4.6 %all-to-all-start.1 = ((f32[64,1,504]{2,1,0:T(1,128)}), f32[64,1,504]{2,1,0:T(1,128)S(1)}, u32[]{:S(2)}, u32[]{:S(2)}) async-start(f32[64,1,504]{2,1,0:T(1,128)} %reshape.4352), calls=%async_computation.1 | async-start | bytes 262144 | tf_op jit(solution)/shard_map/all_to_all | solution.py:120
  65.9 8.1 %all-to-all-done.1 = f32[64,1,504]{2,1,0:T(1,128)S(1)} async-done(((f32[64,1,504]{2,1,0:T(1,128)}), f32[64,1,504]{2,1,0:T(1,128)S(1)}, u32[]{:S(2)}, u32[]{:S(2)}) %all-to-all-start.1) | async-done | bytes 129056 | tf_op jit(solution)/shard_map/all_to_all | solution.py:120
  74.2 2.5 %fusion.62 = f32[1,1,28,12,96]{4,2,3,1,0:T(8,128)S(1)} fusion(s32[12,96]{1,0:T(8,128)S(1)} %multiply_add_fusion.1, s32[18,64]{1,0:T(8,128)S(1)} %copy.80, f32[64,28,18]{0,2,1:T(8,128)S(1)} %reshape.4335, f32[1,1,28,12,96]{4,1,3,2,0:T(1,128)S(1)} %copy-done.1), kind=kOutput, calls=%fused_computation.129 | convolution fusion | flops 447266304 | bytes 396288 | tf_op jit(solution)/shard_map/telp,tpc->elc/dot_general | solution.py:122
  77.1 1.0 copy.83
  78.2 106.6 %while.19 = (s32[]{:T(128)}, f32[8,192]{1,0:T(8,128)S(1)}, f32[8,192]{1,0:T(8,128)S(1)}, f32[16,8,8,192]{3,2,1,0:T(8,128)S(1)}, s32[16,8]{0,1:T(8,128)S(1)}, /*i...) while((s32[]{:T(128)}, f32[8,192]{1,0:T(8,128)S(1)}, ...), condition=%wide.region_7.8_spmd.clone.clone, body=%wide.region_6.7_spmd.clone.clone.sunk | while | flops 228562 | bytes 435795 | solution.py:85
  104.9 0.6 fusion.141
  186.7 0.9 dynamic-slice_bitcast_fusion.1
  190.3 1.1 fusion.80
  191.4 3.5 %copy.99 = f32[16,7,1,12,2,8]{3,5,4,2,1,0:T(8,128)S(1)} copy(f32[16,7,1,12,2,8]{5,4,3,1,2,0:T(2,128)S(1)} %fusion.80) | data formatting | bytes 172032 | tf_op jit(solution)/shard_map/stack | solution.py:142
  194.9 1.3 reshape.4367
  196.2 3.8 %all-to-all-start.2 = ((f32[16,1,1344]{2,1,0:T(1,128)}), f32[16,1,1344]{2,1,0:T(1,128)S(1)}, u32[]{:S(2)}, u32[]{:S(2)}) async-start(f32[16,1,1344]{2,1,0:T(1,128)} %reshape.4367), calls=%async_computation.2 | async-start | bytes 180224 | tf_op jit(solution)/shard_map/all_to_all | solution.py:141
  200.0 0.9 copy.102
  200.8 6.5 %all-to-all-done.2 = f32[16,1,1344]{2,1,0:T(1,128)S(1)} async-done(((f32[16,1,1344]{2,1,0:T(1,128)}), f32[16,1,1344]{2,1,0:T(1,128)S(1)}, u32[]{:S(2)}, u32[]{:S(2)}) %all-to-all-start.2) | async-done | bytes 86048 | tf_op jit(solution)/shard_map/all_to_all | solution.py:141
  207.8 0.9 reduce.16
  210.0 0.9 convolution_bitcast_fusion.1
  210.9 0.7 copy.103
  (343 shorter events, 38.6 us)
Async XLA Ops:
  15.4 11.4 %copy-start.2 = (s32[128]{0:T(128)S(1)}, s32[128]{0:T(128)}, u32[]{:S(2)}) copy-start(s32[128]{0:T(128)} %param.11) | copy-start | bytes 1540
  17.3 19.1 %all-to-all-start = ((f32[64,1,1008]{2,1,0:T(1,128)}), f32[64,1,1008]{2,1,0:T(1,128)S(1)}, u32[]{:S(2)}, u32[]{:S(2)}) async-start(f32[64,1,1008]{2,1,0:T(1,128)} %copy.72), calls=%async_computation | async-start | bytes 524288 | tf_op jit(solution)/shard_map/all_to_all | solution.py:110
  41.5 1.1 copy-start
  59.0 15.2 %copy-start.1 = (f32[1,1,28,12,96]{4,1,3,2,0:T(1,128)S(1)}, f32[1,1,28,12,96]{4,1,3,2,0:T(1,128)}, u32[]{:S(2)}) copy-start(f32[1,1,28,12,96]{4,1,3,2,0:T(1,128)} %param.7) | copy-start | bytes 387076
  60.8 13.2 %all-to-all-start.1 = ((f32[64,1,504]{2,1,0:T(1,128)}), f32[64,1,504]{2,1,0:T(1,128)S(1)}, u32[]{:S(2)}, u32[]{:S(2)}) async-start(f32[64,1,504]{2,1,0:T(1,128)} %reshape.4352), calls=%async_computation.1 | async-start | bytes 262144 | tf_op jit(solution)/shard_map/all_to_all | solution.py:120
  65.5 121.2 %all-reduce.3.cloned.1.call-start = ((), (), s32[]{:S(2)}) async-start(), calls=%async_computation.3 | async-start | bytes 688128
  184.7 0.7 copy-start.3
  196.2 11.2 %all-to-all-start.2 = ((f32[16,1,1344]{2,1,0:T(1,128)}), f32[16,1,1344]{2,1,0:T(1,128)S(1)}, u32[]{:S(2)}, u32[]{:S(2)}) async-start(f32[16,1,1344]{2,1,0:T(1,128)} %reshape.4367), calls=%async_computation.2 | async-start | bytes 180224 | tf_op jit(solution)/shard_map/all_to_all | solution.py:141
Sparse Core Ops, SparseCore 0:
  78.3 49.5 all-reduce.2
